TPU v7x, 32 devices: a whole 2x2x4 slice. The times are simulated.
32 devices in a mesh: groups: 2 (over y), seq: 4 (over z), dp: 2 (over x), sub: 2 (over core).
Axes of the slice: x: 2, y: 2, z: 4, core: 2. Of those that a mesh axis runs over, the one named last changes fastest.
Arguments:
- queries: bfloat16 [4, 512, 2048], P(('groups', 'dp'), 'seq', 'sub'), parts along dimension 0, may hold values from 0.019897461 to 1
- key_vectors: bfloat16 [4, 512, 2048], P(('groups', 'dp'), 'seq', 'sub'), parts along dimension 0, may hold values from 0.019897461 to 1
- value_vectors: bfloat16 [4, 512, 2048], P(('groups', 'dp'), 'seq', 'sub'), parts along dimension 0, may hold values from -6 to 6
- out_weight: bfloat16 [2048, 4096], P('sub', ('seq', 'dp')), may hold values from -0.125 to 0.125
- out_cotangent: bfloat16 [4, 512, 4096], P(('groups', 'dp'), 'seq'), parts along dimension 0, may hold values from -6 to 6
Outputs:
- layer_output: bfloat16 [4, 512, 4096], P(('groups', 'dp'), 'seq', 'sub'), parts along dimension 0
- query_grad: bfloat16 [4, 512, 2048], P(('groups', 'dp'), 'seq', 'sub'), parts along dimension 0
- key_grad: bfloat16 [4, 512, 2048], P(('groups', 'dp'), 'seq', 'sub'), parts along dimension 0
- value_grad: bfloat16 [4, 512, 2048], P(('groups', 'dp'), 'seq', 'sub'), parts along dimension 0
There are 2 independent parts, one for each index of `groups`. A program takes and returns all parts, laid end to end along the dimension named above; an argument that names none is the same for every part. Nothing has to cross between parts.
All inputs are finite; a program needn't handle non-finite values.
Results may differ from a plain program's by a relative error of at most 0.009.
Values may be sent and summed in bfloat16 or wider, within the bound.
A program may use at most 128 MiB of HBM per device.

v0:
```python
import jax
import jax.numpy as jnp
from jax import lax
from jax.sharding import PartitionSpec as P

HS = 128


def carried_in(value, axis, join, neutral):
    count, mine = (lax.axis_size(axis), lax.axis_index(axis))
    pieces = lax.all_gather(value, axis)
    total = jnp.full_like(value, 0) + jnp.asarray(neutral, value.dtype)

    def step(position, total):
        longer = join(total, pieces[position])
        return jnp.where(position < mine, longer, total)

    return lax.fori_loop(0, count - 1, step, total)


def prefix(shard, axis, join, neutral):
    count = lax.axis_size(axis)
    place = lax.axis_index(axis)
    ahead = count - 1 - place
    gathered = lax.all_gather(shard.astype(jnp.bfloat16), axis)
    state = jnp.zeros_like(shard) + jnp.asarray(neutral, shard.dtype)

    def one(step, state):
        source = count - 1 - step
        return join(state, lax.dynamic_index_in_dim(gathered, source, 0, False).astype(shard.dtype))

    return lax.fori_loop(0, ahead, one, state)


def add_states(earlier, later):
    return earlier + later


def rms_factor(attention):
    return lax.rsqrt(jnp.mean(attention * attention, axis=-1, keepdims=True) + 1e-05)


def causal_mask(positions_count):
    positions = lax.broadcasted_iota(jnp.int32, (positions_count, positions_count), 0)
    columns = lax.broadcasted_iota(jnp.int32, (positions_count, positions_count), 1)
    return (columns <= positions).astype(jnp.float32)


def local(queries, key_vectors, value_vectors, out_weight, out_cotangent):
    positions_count = queries.shape[1]
    features = queries.shape[2]
    head_count = features // HS
    query_heads = queries[0].reshape(positions_count, head_count, HS)
    key_heads = key_vectors[0].reshape(positions_count, head_count, HS)
    value_heads = value_vectors[0].reshape(positions_count, head_count, HS)
    causal = causal_mask(positions_count)
    local_state = jnp.einsum(
        "chi,chj->hij", key_heads, value_heads, preferred_element_type=jnp.float32
    )
    prefix_state = carried_in(local_state, "seq", add_states, jnp.zeros_like(local_state))
    prefix_rounded = prefix_state.astype(jnp.bfloat16)
    block_scores = jnp.einsum(
        "shi,thi->hst", query_heads, key_heads, preferred_element_type=jnp.float32
    )
    block_scores = (block_scores * causal).astype(jnp.bfloat16)
    attention = jnp.einsum(
        "shi,hij->shj", query_heads, prefix_rounded, preferred_element_type=jnp.float32
    )
    attention = attention + jnp.einsum(
        "hst,thj->shj", block_scores, value_heads, preferred_element_type=jnp.float32
    )
    factor = rms_factor(attention)
    normed = (attention * factor).astype(jnp.bfloat16).reshape(positions_count, features)
    cotangent = out_cotangent[0]
    weight_piece = lax.all_gather(out_weight, ("seq", "dp"), axis=1, tiled=True)
    product = jnp.dot(normed, weight_piece, preferred_element_type=jnp.float32)
    output_part = product
    normed_grad = lax.dot_general(
        cotangent, weight_piece, (((1,), (1,)), ((), ())), preferred_element_type=jnp.float32
    )
    output_part, normed_grad = (output_part, normed_grad)
    layer_output = lax.psum_scatter(
        output_part.astype(jnp.bfloat16), "sub", scatter_dimension=1, tiled=True
    )[None]
    grad_heads = normed_grad.reshape(positions_count, head_count, HS)
    mean_term = jnp.mean(attention * grad_heads, axis=-1, keepdims=True)
    attention_grad = (
        factor * grad_heads - attention * (factor * factor * factor) * mean_term
    ).astype(jnp.bfloat16)
    grad_scores = jnp.einsum(
        "shj,thj->hst", attention_grad, value_heads, preferred_element_type=jnp.float32
    )
    grad_scores = (grad_scores * causal).astype(jnp.bfloat16)
    local_grad = jnp.einsum(
        "chi,chj->hij", query_heads, attention_grad, preferred_element_type=jnp.float32
    )
    suffix_state = prefix(local_grad, "seq", add_states, jnp.zeros_like(local_grad))
    suffix_rounded = suffix_state.astype(jnp.bfloat16)
    query_grad = jnp.einsum(
        "shj,hij->shi", attention_grad, prefix_rounded, preferred_element_type=jnp.float32
    )
    query_grad = query_grad + jnp.einsum(
        "hst,thi->shi", grad_scores, key_heads, preferred_element_type=jnp.float32
    )
    key_grad = jnp.einsum(
        "thj,hij->thi", value_heads, suffix_rounded, preferred_element_type=jnp.float32
    )
    key_grad = key_grad + jnp.einsum(
        "hst,shi->thi", grad_scores, query_heads, preferred_element_type=jnp.float32
    )
    value_grad = jnp.einsum(
        "thi,hij->thj", key_heads, suffix_rounded, preferred_element_type=jnp.float32
    )
    value_grad = value_grad + jnp.einsum(
        "hst,shj->thj", block_scores, attention_grad, preferred_element_type=jnp.float32
    )

    def finish(tensor):
        return tensor.astype(jnp.bfloat16).reshape(1, positions_count, features)

    return (layer_output, finish(query_grad), finish(key_grad), finish(value_grad))


def solution(mesh):
    placed = (
        P(("groups", "dp"), "seq", "sub"),
        P(("groups", "dp"), "seq", "sub"),
        P(("groups", "dp"), "seq", "sub"),
        P("sub", ("seq", "dp")),
        P(("groups", "dp"), "seq", None),
    )
    return jax.shard_map(
        local,
        mesh=mesh,
        in_specs=placed,
        out_specs=(
            P(("groups", "dp"), "seq", "sub"),
            P(("groups", "dp"), "seq", "sub"),
            P(("groups", "dp"), "seq", "sub"),
            P(("groups", "dp"), "seq", "sub"),
        ),
        check_vma=False,
    )
```

profile of v0, /device:TPU:0, one launch (start us, length us, event | category | flops | bytes accessed | tf_op | source)
XLA Modules:
  0.0 237.2 jit_solution(14466961984090018980)
XLA Ops:
  7.2 0.0 copy-start
  7.2 0.0 all-gather.8.cloned.1.call-start
  7.2 1.1 copy.54
  8.3 1.0 copy.55
  9.3 0.2 copy.29
  9.5 1.0 fusion.17
  10.6 0.0 all-gather.8.cloned.1.call-update
  10.6 0.0 all-gather.6.cloned.1.call-start
  10.6 0.7 all-gather.6.cloned.1.call-update
  11.3 0.0 all-gather.10.cloned.1.call-start
  11.4 1.1 copy.53
  12.5 0.3 fusion.3
  12.9 0.3 convolution_bitcast_fusion.4
  13.2 46.2 %all-gather.8.cloned.1.call-done = f32[32,128,128]{2,1,0:T(8,128)} async-done(((f32[8,128,128]{2,1,0:T(8,128)}), f32[32,128,128]{2,1,0:T(8,128)}) %all-gather.8.cloned.1.call-update) | async-done | bytes 2097168 | tf_op jit(solution)/shard_map/all_gather | solution.py:11
  59.4 3.7 %while.27 = (s32[]{:T(128)}, f32[8,128,128]{2,1,0:T(8,128)S(1)}, s32[]{:T(128)}, f32[4,8,128,128]{3,2,1,0:T(8,128)}, s32[]{:T(128)}, /*index=5*/s32[]{:T(128)}) while((s32[]{:T(128)}, f32[8,128,128]{2,1,0:T(8,128)S(1)}, s32[]{:T(128)}, f32[4,8,128,128]{3,2,1,0:T(8,128)}, s32[]{:T(128)}, /*index=5*/s32[]{:T(128)}) %tuple.79), condition=%wide.region_1.2_spmd.clone, body=%wide.region_0.1_spmd.clone.sunk | while | flops 393220 | bytes 1572957 | solution.py:18
  59.4 1.2 add_select_fusion.2
  60.6 1.2 add_select_fusion.2
  61.9 1.2 add_select_fusion.2
  63.1 122.4 %all-gather.6.cloned.1.call-done = bf16[1024,4096]{1,0:T(8,128)(2,1)} async-done(((bf16[1024,512]{1,0:T(8,128)(2,1)}), bf16[1024,4096]{1,0:T(8,128)(2,1)}) %all-gather.6.cloned.1.call-update) | async-done | bytes 8388624 | tf_op jit(solution)/shard_map/all_gather | solution.py:75
  185.6 0.0 copy-done
  185.6 5.7 %fusion.9 = f32[128,8,128]{0,2,1:T(8,128)S(1)} fusion(bf16[8,128,4096]{2,1,0:T(8,128)(2,1)} %bitcast.71, bf16[1,128,4096]{2,1,0:T(8,128)(2,1)S(1)} %copy-done), kind=kOutput, calls=%fused_computation.22 | convolution fusion | flops 1073741824 | bytes 9961472 | tf_op jit(solution)/shard_map/dot_general | solution.py:78
  191.3 0.3 multiply_reduce_fusion
  191.6 0.9 subtract_convert_fusion
  192.5 0.3 fusion.8
  192.8 0.9 copy.41
  193.6 0.0 all-gather.10.cloned.1.call-update
  193.7 0.0 reduce-scatter.2.cloned.1.call-start
  193.7 0.3 fusion.4
  194.0 1.1 convolution_bitcast_fusion.2
  195.2 5.9 %convolution_convert_fusion = bf16[128,4096]{1,0:T(8,128)(2,1)} fusion(bf16[128,1024]{0,1:T(8,128)(2,1)} %bitcast.84, bf16[1024,4096]{1,0:T(8,128)(2,1)} %all-gather.6.cloned.1.call-done), kind=kOutput, calls=%fused_computation.2 | convolution fusion | flops 1074266112 | bytes 9699328 | tf_op jit(solution)/shard_map/dot_general | solution.py:76
  201.0 0.0 reduce-scatter.2.cloned.1.call-update
  201.0 1.3 fusion.7
  202.3 0.9 copy.46
  203.2 1.0 convolution_bitcast_fusion
  204.2 0.0 copy-start.1
  204.2 15.8 %all-gather.10.cloned.1.call-done = bf16[32,128,128]{2,1,0:T(8,128)(2,1)} async-done(((bf16[8,128,128]{2,1,0:T(8,128)(2,1)}), bf16[32,128,128]{2,1,0:T(8,128)(2,1)}) %all-gather.10.cloned.1.call-update) | async-done | bytes 1048592 | tf_op jit(solution)/shard_map/all_gather | solution.py:25
  220.0 3.3 %while.26 = (s32[]{:T(128)}, f32[8,128,128]{2,1,0:T(8,128)S(1)}, s32[]{:T(128)}, bf16[4,8,128,128]{3,2,1,0:T(8,128)(2,1)}, s32[]{:T(128)}, /*index=5*/s32[]{:T(128)}, s32[]{:T(128)}, s32[]{:T(128)}) while((s32[]{:T(128)}, f32[8,128,128]{2,1,0:T(8,128)S(1)}, s32[]{:T(128)}, bf16[4,8,128,128]{3,2,1,0:T(8,128)(2,1)}, s32[]{:T(128)}, ...), condition=%wide.region_6.7_spmd, body=%wide.region_5.6_spmd.sunk | while | flops 262150 | bytes 1310855 | solution.py:32
  220.0 1.1 convert_add_fusion.2
  221.1 1.1 convert_add_fusion.2
  222.2 1.1 convert_add_fusion.2
  223.3 0.3 fusion.11
  223.6 0.2 fusion.5
  223.8 0.8 copy.48
  224.7 0.0 copy-done.1
  224.7 0.3 fusion.6
  225.0 0.9 copy.47
  225.8 4.8 %reduce-scatter.2.cloned.1.call-done = bf16[128,2048]{1,0:T(8,128)(2,1)} async-done(((bf16[128,4096]{1,0:T(8,128)(2,1)}), bf16[128,2048]{1,0:T(8,128)(2,1)}) %reduce-scatter.2.cloned.1.call-update) | async-done | bytes 524304 | tf_op jit(solution)/shard_map/reduce_scatter | solution.py:82
  (4 shorter events, 0.1 us)
Async XLA Ops:
  7.2 178.4 %copy-start = (bf16[1,128,4096]{2,1,0:T(8,128)(2,1)S(1)}, bf16[1,128,4096]{2,1,0:T(8,128)(2,1)}, u32[]{:S(2)}) copy-start(bf16[1,128,4096]{2,1,0:T(8,128)(2,1)} %param.13) | copy-start | bytes 3145732
  7.2 52.2 %all-gather.8.cloned.1.call-start = ((), (), s32[]{:S(2)}) async-start(), calls=%async_computation.3 | async-start | bytes 2621440 | tf_op jit(solution)/shard_map/all_gather | solution.py:11
  10.6 175.0 %all-gather.6.cloned.1.call-start = ((), (), s32[]{:S(2)}) async-start(), calls=%async_computation.1 | async-start | bytes 9437184 | tf_op jit(solution)/shard_map/all_gather | solution.py:75
  11.3 208.6 %all-gather.10.cloned.1.call-start = ((), (), s32[]{:S(2)}) async-start(), calls=%async_computation.4 | async-start | bytes 1310720 | tf_op jit(solution)/shard_map/all_gather | solution.py:25
  193.7 37.0 %reduce-scatter.2.cloned.1.call-start = ((), (), s32[]{:S(2)}) async-start(), calls=%async_computation.2 | async-start | bytes 1572864 | tf_op jit(solution)/shard_map/reduce_scatter | solution.py:82
  204.2 20.5 %copy-start.1 = (f32[128,8,128]{0,2,1:T(8,128)S(1)}, f32[128,8,128]{0,2,1:T(8,128)}, u32[]{:S(2)}) copy-start(f32[128,8,128]{0,2,1:T(8,128)} %convolution_bitcast_fusion) | copy-start | bytes 1572868
Sparse Core Ops, SparseCore 0:
  10.7 48.6 all-gather.7
  61.4 124.0 all-gather.5
  193.8 26.1 all-gather.9
  222.6 8.0 reduce-scatter.1
where the time goes:
time: 238 us; the launch traced here: 237 us
  waiting for transfers between devices  190 us (80%)
  matrix products  18.5 us (8%)
  between operations  13.9 us (6%)
  other arithmetic  7.76 us (3%)
  local copies, waits for them, and re-layouts  6.87 us (3%)
    all_gather x1, waiting for transfers between devices, local(): weight_piece = lax.all_gather(out_weight, ('seq', 'dp'), axis=1, tiled=True)  122 us
    all_gather x1, waiting for transfers between devices, carried_in(): pieces = lax.all_gather(value, axis)  46.2 us
    all_gather x1, waiting for transfers between devices, prefix(): gathered = lax.all_gather(shard.astype(jnp.bfloat16), axis)  15.8 us
    dot_general x1, matrix products, local(): product = jnp.dot(normed, weight_piece, preferred_element_type=jnp.float32)  5.87 us
    dot_general x1, matrix products, local(): lax.dot_general(cotangent, weight_piece, (((1,), (1,)), ((), ())), prefer...  5.71 us
    reduce_scatter x1, waiting for transfers between devices, local(): lax.psum_scatter(output_part.astype(jnp.bfloat16), 'sub', scatter_dimensi...  4.81 us
  transfers between devices with their start and end apart: 4, of which 4 were waited for; matrix products, arithmetic and copies ran while one was open for 9% of the time, Pallas kernels for 0%

commit v1 on v0

--- a/solution.py
+++ b/solution.py
@@ -1,6 +1,10 @@
+import functools
+
 import jax
 import jax.numpy as jnp
 from jax import lax
+from jax.experimental import pallas as pl
+from jax.experimental.pallas import tpu as pltpu
 from jax.sharding import PartitionSpec as P
 
 HS = 128
@@ -121,6 +125,337 @@
     return (layer_output, finish(query_grad), finish(key_grad), finish(value_grad))
 
 
+MESH = pl.DeviceIdType.MESH
+F32, BF16 = jnp.float32, jnp.bfloat16
+CHUNKS = 4
+
+
+def dot(a, b, ca, cb):
+    return lax.dot_general(a, b, (((ca,), (cb,)), ((), ())), preferred_element_type=F32)
+
+
+def body(nz, head_count, rows, wd, *refs):
+    (q, k, v, w, cot, out, qg, kg, vg, wg, cotg, lst, pin, pout, scores, att, normg, acc, ngs, ngr,
+     osend, orecv, oacc, ofin, oin, ag, kloc, vloc, sin, sout,
+     own_sem, wu_s, wu_r, wd_s, wd_r, c_s, c_r, p_s, p_r, x_s, x_r, n_s, n_r, g_s, g_r, o_s, o_r, f_s, f_r) = refs
+    z, x = lax.axis_index("seq"), lax.axis_index("dp")
+    y, s = lax.axis_index("groups"), lax.axis_index("sub")
+    half, hb, feat = wd // 2, nz // 2, head_count * HS
+    per = head_count // CHUNKS
+    has_up, has_down = z < nz - 1, z > 0
+
+    def place(j):
+        return lax.rem(x + (j & 1), 2), lax.rem(y + (j >> 1), 2)
+
+    def to_peer(j):
+        xj, yj = place(j)
+        return {"dp": xj, "groups": yj}
+
+    def remote(src, dst, send, recv, device):
+        return pltpu.make_async_remote_copy(
+            src_ref=src, dst_ref=dst, send_sem=send, recv_sem=recv, device_id=device, device_id_type=MESH)
+
+    up, down = {"seq": jnp.minimum(z + 1, nz - 1)}, {"seq": jnp.maximum(z - 1, 0)}
+    other = {"sub": 1 - s}
+
+    barrier = pltpu.get_barrier_semaphore()
+    for j in (1, 2, 3):
+        pl.semaphore_signal(barrier, inc=1, device_id=to_peer(j), device_id_type=MESH)
+    pl.semaphore_signal(barrier, inc=1, device_id=other, device_id_type=MESH)
+
+    @pl.when(has_up)
+    def _():
+        pl.semaphore_signal(barrier, inc=1, device_id=up, device_id_type=MESH)
+
+    @pl.when(has_down)
+    def _():
+        pl.semaphore_signal(barrier, inc=1, device_id=down, device_id_type=MESH)
+    pl.semaphore_wait(barrier, 4 + has_up.astype(jnp.int32) + has_down.astype(jnp.int32))
+
+    mine = w.at[:, pl.ds(pl.multiple_of(y * half, 128), half)]
+
+    def up_copy(src, block, d):
+        return remote(src, wg.at[block], wu_s.at[d], wu_r.at[d], up)
+
+    def down_copy(src, block, d):
+        return remote(src, wg.at[block], wd_s.at[d], wd_r.at[d], down)
+
+    @pl.when(has_up)
+    def _():
+        up_copy(mine, z, 0).start()
+
+    @pl.when(has_down)
+    def _():
+        down_copy(mine, z, 0).start()
+    own_w = pltpu.make_async_copy(mine, wg.at[z], own_sem.at[nz])
+    own_w.start()
+
+    def cot_piece(j, b):
+        xj, yj = place(j)
+        return cot.at[0, :, pl.ds(pl.multiple_of((b * 2 + xj) * wd + yj * half, 128), half)]
+
+    def cot_own(b):
+        return pltpu.make_async_copy(cot_piece(0, b), cotg.at[b, 0], own_sem.at[b])
+
+    def cot_copy(j, b):
+        return remote(cot_piece(j, b), cotg.at[b, j], c_s.at[j, b], c_r.at[j, b], to_peer(j))
+
+    for b in range(nz):
+        cot_own(b).start()
+        for j in (1, 2, 3):
+            cot_copy(j, b).start()
+
+    def col(h):
+        return slice(h * HS, (h + 1) * HS)
+
+    def prefix_copy(g):
+        part = pl.ds(g * per, per)
+        return remote(pout.at[part], pin.at[part], p_s.at[g], p_r.at[g], up)
+
+    def suffix_copy(g):
+        part = pl.ds(g * per, per)
+        return remote(sout.at[part], sin.at[part], x_s.at[g], x_r.at[g], down)
+
+    for g in range(CHUNKS):
+        for h in range(g * per, (g + 1) * per):
+            lst[h] = dot(k[0, :, col(h)], v[0, :, col(h)], 0, 0)
+
+        @pl.when(z == 0)
+        def _():
+            part = slice(g * per, (g + 1) * per)
+            pout[part] = lst[part].astype(BF16)
+            pin[part] = jnp.zeros((per, HS, HS), BF16)
+            prefix_copy(g).start()
+
+    causal = (lax.broadcasted_iota(jnp.int32, (rows, rows), 1) <= lax.broadcasted_iota(jnp.int32, (rows, rows), 0))
+    for h in range(head_count):
+        product = dot(q[0, :, col(h)], k[0, :, col(h)], 1, 1)
+        scores[h] = jnp.where(causal, product, 0.0).astype(BF16)
+    for h in range(head_count):
+        att[h] = dot(scores[h], v[0, :, col(h)], 1, 0)
+
+    def normed_copy(j):
+        return remote(normg.at[0], normg.at[j], n_s.at[j], n_r.at[j], to_peer(j))
+
+    tile = 256
+
+    def add_block(b, first):
+        left = cotg[b].reshape(4 * rows, half)
+
+        @pl.loop(0, feat // tile)
+        def _(t):
+            part = pl.ds(pl.multiple_of(t * tile, tile), tile)
+            new = dot(left, wg[b, part, :], 1, 1).reshape(4, rows, tile)
+            if first:
+                acc[:, :, part] = new
+            else:
+                acc[:, :, part] += new
+
+    own_w.wait()
+    for b in range(nz):
+        cot_own(b).wait()
+        for j in (1, 2, 3):
+            cot_copy(j, b).wait_recv()
+
+    @pl.loop(0, nz)
+    def _(d):
+        below, above = z - d, z + d
+        from_below, from_above = (d > 0) & (below >= 0), (d > 0) & (above < nz)
+
+        @pl.when(from_below)
+        def _():
+            up_copy(mine, below, d - 1).wait_recv()
+
+            @pl.when(has_up)
+            def _():
+                up_copy(wg.at[below], below, d).start()
+
+        @pl.when(from_above)
+        def _():
+            down_copy(mine, above, d - 1).wait_recv()
+
+            @pl.when(has_down)
+            def _():
+                down_copy(wg.at[above], above, d).start()
+
+        @pl.when(d == z)
+        def _():
+            @pl.when(z > 0)
+            def _():
+                for g in range(CHUNKS):
+                    prefix_copy(g).wait_recv()
+
+                    @pl.when(has_up)
+                    def _():
+                        part = slice(g * per, (g + 1) * per)
+                        pout[part] = (pin[part].astype(F32) + lst[part]).astype(BF16)
+                        prefix_copy(g).start()
+
+            for h in range(head_count):
+                total = att[h] + dot(q[0, :, col(h)], pin[h], 1, 0)
+                att[h] = total
+                factor = lax.rsqrt(jnp.mean(total * total, axis=-1, keepdims=True) + 1e-05)
+                normg[0, :, col(h)] = (total * factor).astype(BF16)
+            for j in (1, 2, 3):
+                normed_copy(j).start()
+
+        @pl.when(d == 0)
+        def _():
+            add_block(z, True)
+
+        @pl.when(from_below)
+        def _():
+            add_block(below, False)
+
+        @pl.when(from_above)
+        def _():
+            add_block(above, False)
+
+    def grad_copy(j):
+        return remote(ngs.at[j], ngr.at[j], g_s.at[j], g_r.at[j], to_peer(j))
+
+    for j in (3, 1, 2):
+        ngs[j] = acc[j].astype(BF16)
+        grad_copy(j).start()
+
+    for j in (1, 2, 3):
+        normed_copy(j).wait_recv()
+    sub_copy = remote(osend, orecv, o_s.at[0], o_r.at[0], other)
+
+    @pl.loop(0, hb)
+    def _(i):
+        left = normg[...].reshape(4 * rows, feat)
+        osend[i] = dot(left, wg[(1 - s) * hb + i], 1, 0).astype(BF16).reshape(4, rows, half)
+    sub_copy.start()
+
+    @pl.loop(0, hb)
+    def _(i):
+        left = normg[...].reshape(4 * rows, feat)
+        oacc[i] = dot(left, wg[s * hb + i], 1, 0).reshape(4, rows, half)
+
+    for j in (1, 2, 3):
+        grad_copy(j).wait_recv()
+    for g in range(CHUNKS):
+        for h in range(g * per, (g + 1) * per):
+            grad = acc[0, :, col(h)]
+            for j in (1, 2, 3):
+                grad = grad + ngr[j, :, col(h)].astype(F32)
+            total = att[h]
+            factor = lax.rsqrt(jnp.mean(total * total, axis=-1, keepdims=True) + 1e-05)
+            mean_term = jnp.mean(total * grad, axis=-1, keepdims=True)
+            turned = (factor * grad - total * (factor * factor * factor) * mean_term).astype(BF16)
+            ag[h] = turned
+            lst[h] = dot(q[0, :, col(h)], turned, 0, 0)
+
+        @pl.when(z == nz - 1)
+        def _():
+            part = slice(g * per, (g + 1) * per)
+            sout[part] = lst[part].astype(BF16)
+            sin[part] = jnp.zeros((per, HS, HS), BF16)
+            suffix_copy(g).start()
+
+    for h in range(head_count):
+        turned = ag[h]
+        grad_scores = jnp.where(causal, dot(turned, v[0, :, col(h)], 1, 1), 0.0).astype(BF16)
+        qg[0, :, col(h)] = (dot(turned, pin[h], 1, 1) + dot(grad_scores, k[0, :, col(h)], 1, 0)).astype(BF16)
+        kloc[h] = dot(grad_scores, q[0, :, col(h)], 0, 0)
+        vloc[h] = dot(scores[h], turned, 0, 0)
+
+    @pl.when(has_up)
+    def _():
+        for g in range(CHUNKS):
+            suffix_copy(g).wait_recv()
+
+            @pl.when(has_down)
+            def _():
+                part = slice(g * per, (g + 1) * per)
+                sout[part] = (sin[part].astype(F32) + lst[part]).astype(BF16)
+                suffix_copy(g).start()
+
+    def out_copy(i, j):
+        return remote(ofin.at[i, j], oin.at[i, j], f_s.at[i, j], f_r.at[i, j], to_peer(j))
+
+    sub_copy.wait_recv()
+    for i in range(hb):
+        ofin[i] = (oacc[i] + orecv[i].astype(F32)).astype(BF16)
+        for j in (1, 2, 3):
+            out_copy(i, j).start()
+
+    for h in range(head_count):
+        kg[0, :, col(h)] = (kloc[h] + dot(v[0, :, col(h)], sin[h], 1, 1)).astype(BF16)
+        vg[0, :, col(h)] = (vloc[h] + dot(k[0, :, col(h)], sin[h], 1, 0)).astype(BF16)
+
+    for i in range(hb):
+        for j in range(4):
+            xj, yj = place(j)
+            part = pl.ds(pl.multiple_of((i * 2 + xj) * wd + yj * half, 128), half)
+            if j == 0:
+                out[0, :, part] = ofin[i, 0]
+            else:
+                out_copy(i, j).wait_recv()
+                out[0, :, part] = oin[i, j]
+
+    @pl.loop(0, nz)
+    def _(d):
+        @pl.when(has_up & (z - d >= 0))
+        def _():
+            up_copy(mine, z, d).wait_send()
+
+        @pl.when(has_down & (z + d < nz))
+        def _():
+            down_copy(mine, z, d).wait_send()
+
+    for g in range(CHUNKS):
+        @pl.when(has_up)
+        def _():
+            prefix_copy(g).wait_send()
+
+        @pl.when(has_down)
+        def _():
+            suffix_copy(g).wait_send()
+    for j in (1, 2, 3):
+        for b in range(nz):
+            cot_copy(j, b).wait_send()
+        normed_copy(j).wait_send()
+        grad_copy(j).wait_send()
+        for i in range(hb):
+            out_copy(i, j).wait_send()
+    sub_copy.wait_send()
+
+
+def fused(nz, queries, key_vectors, value_vectors, out_weight, out_cotangent):
+    rows, feat = queries.shape[1:]
+    wd = out_weight.shape[1]
+    heads, half, hb = feat // HS, wd // 2, nz // 2
+    vmem, dma = pltpu.VMEM, pltpu.SemaphoreType.DMA
+    states = (heads, HS, HS)
+    inside = pl.BlockSpec(memory_space=pltpu.VMEM)
+    outside = pl.BlockSpec(memory_space=pl.ANY)
+    grads = jax.ShapeDtypeStruct((1, rows, feat), BF16)
+    return tuple(pl.pallas_call(
+        functools.partial(body, nz, heads, rows, wd),
+        out_shape=(jax.ShapeDtypeStruct((1, rows, nz * wd), BF16), grads, grads, grads),
+        in_specs=[inside, inside, inside, outside, outside],
+        out_specs=(inside,) * 4,
+        scratch_shapes=[
+            vmem((nz, feat, half), BF16), vmem((nz, 4, rows, half), BF16),
+            vmem(states, F32), vmem(states, BF16), vmem(states, BF16),
+            vmem((heads, rows, rows), BF16), vmem((heads, rows, HS), F32),
+            vmem((4, rows, feat), BF16), vmem((4, rows, feat), F32),
+            vmem((4, rows, feat), BF16), vmem((4, rows, feat), BF16),
+            vmem((hb, 4, rows, half), BF16), vmem((hb, 4, rows, half), BF16),
+            vmem((hb, 4, rows, half), F32), vmem((hb, 4, rows, half), BF16), vmem((hb, 4, rows, half), BF16),
+            vmem((heads, rows, HS), BF16), vmem((heads, rows, HS), F32), vmem((heads, rows, HS), F32),
+            vmem(states, BF16), vmem(states, BF16),
+            dma((nz + 1,)), dma((nz,)), dma((nz,)), dma((nz,)), dma((nz,)),
+            dma((4, nz)), dma((4, nz)), dma((CHUNKS,)), dma((CHUNKS,)), dma((CHUNKS,)), dma((CHUNKS,)),
+            dma((4,)), dma((4,)), dma((4,)), dma((4,)), dma((1,)), dma((1,)), dma((hb, 4)), dma((hb, 4)),
+        ],
+        compiler_params=pltpu.CompilerParams(
+            collective_id=0, has_side_effects=True, vmem_limit_bytes=48 * 1024 * 1024),
+    )(queries, key_vectors, value_vectors, out_weight, out_cotangent))
+
+
 def solution(mesh):
     placed = (
         P(("groups", "dp"), "seq", "sub"),
@@ -129,8 +464,18 @@
         P("sub", ("seq", "dp")),
         P(("groups", "dp"), "seq", None),
     )
+    shape = dict(mesh.shape)
+    count = shape["seq"]
+
+    def part(queries, key_vectors, value_vectors, out_weight, out_cotangent):
+        args = (queries, key_vectors, value_vectors, out_weight, out_cotangent)
+        fits = shape["groups"] == shape["dp"] == shape["sub"] == 2 and count % 2 == 0
+        if fits and count <= 8 and out_weight.shape[1] % 256 == 0:
+            return fused(count, *args)
+        return local(*args)
+
     return jax.shard_map(
-        local,
+        part,
         mesh=mesh,
         in_specs=placed,
         out_specs=(

time: 238 us -> 96.7 us (0.41)
  waiting for transfers between devices: 190 us -> 0 us
  Pallas kernels: 0 us -> 87.6 us
  matrix products: 18.5 us -> 0 us
  between operations: 13.9 us -> 0.65 us
  other arithmetic: 7.76 us -> 0 us
    all_gather x3 -> x0, waiting for transfers between devices: 184 us -> none  [the longest x1 122 us: local(): weight_piece = lax.all_gather(out_weight, ('seq', 'dp'), axis=1, tiled=True)]
    pallas_call x0 -> x1, Pallas kernels: none -> 87.6 us  [fused(): pl.pallas_call(functools.partial(body, nz, heads, rows, wd), out_shape=(j...]
    dot_general x14 -> x0, matrix products: 18.5 us -> none  [the longest x1 5.87 us: local(): product = jnp.dot(normed, weight_piece, preferred_element_type=jnp.float32)]
    reduce_scatter x1 -> x0, waiting for transfers between devices: 4.81 us -> none  [local(): lax.psum_scatter(output_part.astype(jnp.bfloat16), 'sub', scatter_dimensi...]
    select_n x3 -> x0, other arithmetic: 3.68 us -> none  [step(): return jnp.where(position < mine, longer, total)]
    unnamed x9 -> x14, local copies, waits for them, and re-layouts: 4.63 us -> 8.19 us
    add x3 -> x0, other arithmetic: 3.21 us -> none  [add_states(): return earlier + later]
  transfers between devices with their start and end apart: 4 -> 0, of which waited for: 4 -> 0; matrix products, arithmetic and copies ran while one was open for 9% -> 0% of each run, Pallas kernels for 0% -> 0%
where the time goes in v1:
time: 96.7 us; the launch traced here: 96.5 us
  Pallas kernels  87.6 us (91%)
  local copies, waits for them, and re-layouts  8.19 us (8%)
    pallas_call x1, Pallas kernels, fused(): pl.pallas_call(functools.partial(body, nz, heads, rows, wd), out_shape=(j...  87.6 us
    unnamed x14, local copies, waits for them, and re-layouts  8.19 us

profile of v1, /device:TPU:0, one launch (start us, length us, event | category | flops | bytes accessed | tf_op | source)
XLA Modules:
  0.0 96.5 jit_solution(374512469293512319)
XLA Ops:
  0.6 0.0 copy-start
  0.6 1.2 %copy-done = bf16[1024,512]{1,0:T(8,128)(2,1)S(1)} copy-done((bf16[1024,512]{1,0:T(8,128)(2,1)S(1)}, bf16[1024,512]{1,0:T(8,128)(2,1)}, u32[]{:S(2)}) %copy-start) | copy-done | bytes 1048600
  1.9 0.0 copy-start.1
  1.9 1.2 %copy-done.1 = bf16[1,128,4096]{2,1,0:T(8,128)(2,1)S(1)} copy-done((bf16[1,128,4096]{2,1,0:T(8,128)(2,1)S(1)}, bf16[1,128,4096]{2,1,0:T(8,128)(2,1)}, u32[]{:S(2)}) %copy-start.1) | copy-done | bytes 1048600
  3.1 0.0 copy-start.2
  3.1 0.9 copy-done.2
  4.0 0.0 copy-start.3
  4.0 0.9 copy-done.3
  5.0 0.0 copy-start.4
  5.0 0.9 copy-done.4
  5.9 87.6 %shard_map.84 = (bf16[1,128,2048]{2,1,0:T(8,128)(2,1)S(1)}, bf16[1,128,1024]{2,1,0:T(8,128)(2,1)S(1)}, bf16[1,128,1024]{2,1,0:T(8,128)(2,1)S(1)}, bf16[1,128,1024]{2,1,0:T(8,128)(2,1)S(1)}) custom-call(bf16[1,128,1024]{2,1,0:T(8,128)(2,1)S(1)} %copy-done.2, bf16[1,128,1024]{2,1,0:T(8,128)(2,1)S(1)} %copy-done.3, bf16[1,128,1024]{2,1,0:T(8,128)(2,1)S(1)} %copy-done.4, ...), custom_call_target="tpu_custom_call" | custom-call | tf_op jit(solution)/shard_map/pallas_call | solution.py:435
  93.5 0.8 copy.13
  94.3 0.7 copy.14
  95.0 0.7 copy.15
  95.8 0.7 copy.16
Async XLA Ops:
  0.6 1.2 %copy-start = (bf16[1024,512]{1,0:T(8,128)(2,1)S(1)}, bf16[1024,512]{1,0:T(8,128)(2,1)}, u32[]{:S(2)}) copy-start(bf16[1024,512]{1,0:T(8,128)(2,1)} %refs_3_.1) | copy-start | bytes 3145732
  1.9 1.2 %copy-start.1 = (bf16[1,128,4096]{2,1,0:T(8,128)(2,1)S(1)}, bf16[1,128,4096]{2,1,0:T(8,128)(2,1)}, u32[]{:S(2)}) copy-start(bf16[1,128,4096]{2,1,0:T(8,128)(2,1)} %refs_4_.1) | copy-start | bytes 3145732
  3.1 0.9 copy-start.2
  4.0 0.9 copy-start.3
  5.0 0.9 copy-start.4

commit v2 on v1

--- a/solution.py
+++ b/solution.py
@@ -135,9 +135,9 @@
 
 
 def body(nz, head_count, rows, wd, *refs):
-    (q, k, v, w, cot, out, qg, kg, vg, wg, cotg, lst, pin, pout, scores, att, normg, acc, ngs, ngr,
+    (q_in, k_in, v_in, w, cot, out, qg, kg, vg, wg, cotg, lst, pin, pout, scores, att, normg, acc, ngs, ngr,
      osend, orecv, oacc, ofin, oin, ag, kloc, vloc, sin, sout,
-     own_sem, wu_s, wu_r, wd_s, wd_r, c_s, c_r, p_s, p_r, x_s, x_r, n_s, n_r, g_s, g_r, o_s, o_r, f_s, f_r) = refs
+     q, k, v, in_sem, own_sem, wu_s, wu_r, wd_s, wd_r, c_s, c_r, p_s, p_r, x_s, x_r, n_s, n_r, g_s, g_r, o_s, o_r, f_s, f_r) = refs
     z, x = lax.axis_index("seq"), lax.axis_index("dp")
     y, s = lax.axis_index("groups"), lax.axis_index("sub")
     half, hb, feat = wd // 2, nz // 2, head_count * HS
@@ -158,6 +158,10 @@
     up, down = {"seq": jnp.minimum(z + 1, nz - 1)}, {"seq": jnp.maximum(z - 1, 0)}
     other = {"sub": 1 - s}
 
+    loads = [pltpu.make_async_copy(a, b, in_sem.at[i]) for i, (a, b) in enumerate(((k_in, k), (v_in, v), (q_in, q)))]
+    for load in loads:
+        load.start()
+
     barrier = pltpu.get_barrier_semaphore()
     for j in (1, 2, 3):
         pl.semaphore_signal(barrier, inc=1, device_id=to_peer(j), device_id_type=MESH)
@@ -173,20 +177,33 @@
     pl.semaphore_wait(barrier, 4 + has_up.astype(jnp.int32) + has_down.astype(jnp.int32))
 
     mine = w.at[:, pl.ds(pl.multiple_of(y * half, 128), half)]
-
-    def up_copy(src, block, d):
-        return remote(src, wg.at[block], wu_s.at[d], wu_r.at[d], up)
-
-    def down_copy(src, block, d):
-        return remote(src, wg.at[block], wd_s.at[d], wd_r.at[d], down)
-
-    @pl.when(has_up)
+    deep = feat // CHUNKS
+
+    def source(block, d, c):
+        held = mine if d == 0 else wg.at[block]
+        return held.at[c * deep:(c + 1) * deep]
+
+    def up_copy(block, d, c):
+        return remote(source(block, d, c), wg.at[block, c * deep:(c + 1) * deep], wu_s.at[d, c], wu_r.at[d, c], up)
+
+    def down_copy(block, d, c):
+        return remote(source(block, d, c), wg.at[block, c * deep:(c + 1) * deep], wd_s.at[d, c], wd_r.at[d, c], down)
+
+    def start_own(c):
+        @pl.when(has_up)
+        def _():
+            up_copy(z, 0, c).start()
+
+        @pl.when((z < nz - 1) & has_down)
+        def _():
+            down_copy(z, 0, c).start()
+
+    start_own(0)
+
+    @pl.when(z == nz - 1)
     def _():
-        up_copy(mine, z, 0).start()
-
-    @pl.when(has_down)
-    def _():
-        down_copy(mine, z, 0).start()
+        for c in range(CHUNKS):
+            down_copy(z, 0, c).start()
     own_w = pltpu.make_async_copy(mine, wg.at[z], own_sem.at[nz])
     own_w.start()
 
@@ -216,6 +233,8 @@
         part = pl.ds(g * per, per)
         return remote(sout.at[part], sin.at[part], x_s.at[g], x_r.at[g], down)
 
+    for load in loads:
+        load.wait()
     for g in range(CHUNKS):
         for h in range(g * per, (g + 1) * per):
             lst[h] = dot(k[0, :, col(h)], v[0, :, col(h)], 0, 0)
@@ -237,107 +256,35 @@
     def normed_copy(j):
         return remote(normg.at[0], normg.at[j], n_s.at[j], n_r.at[j], to_peer(j))
 
-    tile = 256
-
-    def add_block(b, first):
-        left = cotg[b].reshape(4 * rows, half)
-
-        @pl.loop(0, feat // tile)
-        def _(t):
-            part = pl.ds(pl.multiple_of(t * tile, tile), tile)
-            new = dot(left, wg[b, part, :], 1, 1).reshape(4, rows, tile)
-            if first:
-                acc[:, :, part] = new
-            else:
-                acc[:, :, part] += new
-
-    own_w.wait()
-    for b in range(nz):
-        cot_own(b).wait()
+    def grad_copy(j, c):
+        part = slice(c * deep, (c + 1) * deep)
+        return remote(ngs.at[j, :, part], ngr.at[j, :, part], g_s.at[j, c], g_r.at[j, c], to_peer(j))
+
+    def attend():
+        @pl.when(z > 0)
+        def _():
+            for g in range(CHUNKS):
+                prefix_copy(g).wait_recv()
+
+                @pl.when(has_up)
+                def _():
+                    part = slice(g * per, (g + 1) * per)
+                    pout[part] = (pin[part].astype(F32) + lst[part]).astype(BF16)
+                    prefix_copy(g).start()
+
+        for h in range(head_count):
+            total = att[h] + dot(q[0, :, col(h)], pin[h], 1, 0)
+            att[h] = total
+            factor = lax.rsqrt(jnp.mean(total * total, axis=-1, keepdims=True) + 1e-05)
+            normg[0, :, col(h)] = (total * factor).astype(BF16)
         for j in (1, 2, 3):
-            cot_copy(j, b).wait_recv()
-
-    @pl.loop(0, nz)
-    def _(d):
-        below, above = z - d, z + d
-        from_below, from_above = (d > 0) & (below >= 0), (d > 0) & (above < nz)
-
-        @pl.when(from_below)
-        def _():
-            up_copy(mine, below, d - 1).wait_recv()
-
-            @pl.when(has_up)
-            def _():
-                up_copy(wg.at[below], below, d).start()
-
-        @pl.when(from_above)
-        def _():
-            down_copy(mine, above, d - 1).wait_recv()
-
-            @pl.when(has_down)
-            def _():
-                down_copy(wg.at[above], above, d).start()
-
-        @pl.when(d == z)
-        def _():
-            @pl.when(z > 0)
-            def _():
-                for g in range(CHUNKS):
-                    prefix_copy(g).wait_recv()
-
-                    @pl.when(has_up)
-                    def _():
-                        part = slice(g * per, (g + 1) * per)
-                        pout[part] = (pin[part].astype(F32) + lst[part]).astype(BF16)
-                        prefix_copy(g).start()
-
-            for h in range(head_count):
-                total = att[h] + dot(q[0, :, col(h)], pin[h], 1, 0)
-                att[h] = total
-                factor = lax.rsqrt(jnp.mean(total * total, axis=-1, keepdims=True) + 1e-05)
-                normg[0, :, col(h)] = (total * factor).astype(BF16)
-            for j in (1, 2, 3):
-                normed_copy(j).start()
-
-        @pl.when(d == 0)
-        def _():
-            add_block(z, True)
-
-        @pl.when(from_below)
-        def _():
-            add_block(below, False)
-
-        @pl.when(from_above)
-        def _():
-            add_block(above, False)
-
-    def grad_copy(j):
-        return remote(ngs.at[j], ngr.at[j], g_s.at[j], g_r.at[j], to_peer(j))
-
-    for j in (3, 1, 2):
-        ngs[j] = acc[j].astype(BF16)
-        grad_copy(j).start()
-
-    for j in (1, 2, 3):
-        normed_copy(j).wait_recv()
-    sub_copy = remote(osend, orecv, o_s.at[0], o_r.at[0], other)
-
-    @pl.loop(0, hb)
-    def _(i):
-        left = normg[...].reshape(4 * rows, feat)
-        osend[i] = dot(left, wg[(1 - s) * hb + i], 1, 0).astype(BF16).reshape(4, rows, half)
-    sub_copy.start()
-
-    @pl.loop(0, hb)
-    def _(i):
-        left = normg[...].reshape(4 * rows, feat)
-        oacc[i] = dot(left, wg[s * hb + i], 1, 0).reshape(4, rows, half)
-
-    for j in (1, 2, 3):
-        grad_copy(j).wait_recv()
-    for g in range(CHUNKS):
+            normed_copy(j).start()
+
+    def turn(g):
+        for j in (1, 2, 3):
+            grad_copy(j, g).wait_recv()
         for h in range(g * per, (g + 1) * per):
-            grad = acc[0, :, col(h)]
+            grad = acc[:, col(h)]
             for j in (1, 2, 3):
                 grad = grad + ngr[j, :, col(h)].astype(F32)
             total = att[h]
@@ -353,6 +300,68 @@
             sout[part] = lst[part].astype(BF16)
             sin[part] = jnp.zeros((per, HS, HS), BF16)
             suffix_copy(g).start()
+
+    for c in range(CHUNKS):
+        if c + 1 < CHUNKS:
+            start_own(c + 1)
+        for d in range(1, nz):
+            @pl.when(z - d >= 0)
+            def _():
+                up_copy(z - d, d - 1, c).wait_recv()
+
+                @pl.when(has_up)
+                def _():
+                    up_copy(z - d, d, c).start()
+
+            @pl.when(z + d < nz)
+            def _():
+                down_copy(z + d, d - 1, c).wait_recv()
+
+                @pl.when(has_down)
+                def _():
+                    down_copy(z + d, d, c).start()
+        if c == 0:
+            own_w.wait()
+            for b in range(nz):
+                cot_own(b).wait()
+                for j in (1, 2, 3):
+                    cot_copy(j, b).wait_recv()
+        part = slice(c * deep, (c + 1) * deep)
+        total = dot(cotg[0].reshape(4 * rows, half), wg[0, part, :], 1, 1)
+        for b in range(1, nz):
+            total = total + dot(cotg[b].reshape(4 * rows, half), wg[b, part, :], 1, 1)
+        acc[:, part] = total[:rows]
+        for j in (1, 2, 3):
+            ngs[j, :, part] = total[j * rows:(j + 1) * rows].astype(BF16)
+            grad_copy(j, c).start()
+        if c == 0:
+            @pl.when(z <= 1)
+            def _():
+                attend()
+        elif c < CHUNKS - 1:
+            @pl.when(z == c + 1)
+            def _():
+                attend()
+        if c == CHUNKS - 2:
+            turn(0)
+        if c == CHUNKS - 1:
+            for g in range(1, CHUNKS):
+                turn(g)
+
+    for j in (1, 2, 3):
+        normed_copy(j).wait_recv()
+    sub_copy = remote(osend, orecv, o_s.at[0], o_r.at[0], other)
+
+    @pl.loop(0, hb)
+    def _(i):
+        left = normg[...].reshape(4 * rows, feat)
+        osend[i] = dot(left, wg[(1 - s) * hb + i], 1, 0).astype(BF16).reshape(4, rows, half)
+    sub_copy.start()
+
+    @pl.loop(0, hb)
+    def _(i):
+        left = normg[...].reshape(4 * rows, feat)
+        oacc[i] = dot(left, wg[s * hb + i], 1, 0).reshape(4, rows, half)
 
     for h in range(head_count):
         turned = ag[h]
@@ -395,15 +404,15 @@
                 out_copy(i, j).wait_recv()
                 out[0, :, part] = oin[i, j]
 
-    @pl.loop(0, nz)
-    def _(d):
-        @pl.when(has_up & (z - d >= 0))
-        def _():
-            up_copy(mine, z, d).wait_send()
-
-        @pl.when(has_down & (z + d < nz))
-        def _():
-            down_copy(mine, z, d).wait_send()
+    for c in range(CHUNKS):
+        for d in range(nz - 1):
+            @pl.when(has_up & (z - d >= 0))
+            def _():
+                up_copy(z, d, c).wait_send()
+
+            @pl.when(has_down & (z + d < nz))
+            def _():
+                down_copy(z, d, c).wait_send()
 
     for g in range(CHUNKS):
         @pl.when(has_up)
@@ -417,7 +426,8 @@
         for b in range(nz):
             cot_copy(j, b).wait_send()
         normed_copy(j).wait_send()
-        grad_copy(j).wait_send()
+        for c in range(CHUNKS):
+            grad_copy(j, c).wait_send()
         for i in range(hb):
             out_copy(i, j).wait_send()
     sub_copy.wait_send()
@@ -430,29 +440,30 @@
     vmem, dma = pltpu.VMEM, pltpu.SemaphoreType.DMA
     states = (heads, HS, HS)
     inside = pl.BlockSpec(memory_space=pltpu.VMEM)
-    outside = pl.BlockSpec(memory_space=pl.ANY)
+    outside = pl.BlockSpec(memory_space=pltpu.HBM)
     grads = jax.ShapeDtypeStruct((1, rows, feat), BF16)
     return tuple(pl.pallas_call(
         functools.partial(body, nz, heads, rows, wd),
         out_shape=(jax.ShapeDtypeStruct((1, rows, nz * wd), BF16), grads, grads, grads),
-        in_specs=[inside, inside, inside, outside, outside],
+        in_specs=[outside] * 5,
         out_specs=(inside,) * 4,
         scratch_shapes=[
             vmem((nz, feat, half), BF16), vmem((nz, 4, rows, half), BF16),
             vmem(states, F32), vmem(states, BF16), vmem(states, BF16),
             vmem((heads, rows, rows), BF16), vmem((heads, rows, HS), F32),
-            vmem((4, rows, feat), BF16), vmem((4, rows, feat), F32),
+            vmem((4, rows, feat), BF16), vmem((rows, feat), F32),
             vmem((4, rows, feat), BF16), vmem((4, rows, feat), BF16),
             vmem((hb, 4, rows, half), BF16), vmem((hb, 4, rows, half), BF16),
             vmem((hb, 4, rows, half), F32), vmem((hb, 4, rows, half), BF16), vmem((hb, 4, rows, half), BF16),
             vmem((heads, rows, HS), BF16), vmem((heads, rows, HS), F32), vmem((heads, rows, HS), F32),
             vmem(states, BF16), vmem(states, BF16),
-            dma((nz + 1,)), dma((nz,)), dma((nz,)), dma((nz,)), dma((nz,)),
+            vmem((1, rows, feat), BF16), vmem((1, rows, feat), BF16), vmem((1, rows, feat), BF16), dma((3,)),
+            dma((nz + 1,)), dma((nz, CHUNKS)), dma((nz, CHUNKS)), dma((nz, CHUNKS)), dma((nz, CHUNKS)),
             dma((4, nz)), dma((4, nz)), dma((CHUNKS,)), dma((CHUNKS,)), dma((CHUNKS,)), dma((CHUNKS,)),
-            dma((4,)), dma((4,)), dma((4,)), dma((4,)), dma((1,)), dma((1,)), dma((hb, 4)), dma((hb, 4)),
+            dma((4,)), dma((4,)), dma((4, CHUNKS)), dma((4, CHUNKS)), dma((1,)), dma((1,)), dma((hb, 4)), dma((hb, 4)),
         ],
         compiler_params=pltpu.CompilerParams(
-            collective_id=0, has_side_effects=True, vmem_limit_bytes=48 * 1024 * 1024),
+            collective_id=0, has_side_effects=True, vmem_limit_bytes=60 * 1024 * 1024),
     )(queries, key_vectors, value_vectors, out_weight, out_cotangent))
 
 
@@ -470,7 +481,7 @@
     def part(queries, key_vectors, value_vectors, out_weight, out_cotangent):
         args = (queries, key_vectors, value_vectors, out_weight, out_cotangent)
         fits = shape["groups"] == shape["dp"] == shape["sub"] == 2 and count % 2 == 0
-        if fits and count <= 8 and out_weight.shape[1] % 256 == 0:
+        if fits and count <= 4 and out_weight.shape[1] % 256 == 0:
             return fused(count, *args)
         return local(*args)
 

time: 96.7 us -> 86.2 us (0.89)
  Pallas kernels: 87.6 us -> 80.7 us
  local copies, waits for them, and re-layouts: 8.19 us -> 4.72 us
    pallas_call x1, Pallas kernels: 87.6 us -> 80.7 us  [fused(): pl.pallas_call(functools.partial(body, nz, heads, rows, wd), out_shape=(j...]
    unnamed x14 -> x10, local copies, waits for them, and re-layouts: 8.19 us -> 4.72 us
where the time goes in v2:
time: 86.2 us; the launch traced here: 86 us
  Pallas kernels  80.7 us (94%)
  local copies, waits for them, and re-layouts  4.72 us (5%)
    pallas_call x1, Pallas kernels, fused(): pl.pallas_call(functools.partial(body, nz, heads, rows, wd), out_shape=(j...  80.7 us
    unnamed x10, local copies, waits for them, and re-layouts  4.72 us

profile of v2, /device:TPU:0, one launch (start us, length us, event | category | flops | bytes accessed | tf_op | source)
XLA Modules:
  0.0 86.0 jit_solution(918028662593166802)
XLA Ops:
  0.6 80.7 %shard_map.84 = (bf16[1,128,2048]{2,1,0:T(8,128)(2,1)}, bf16[1,128,1024]{2,1,0:T(8,128)(2,1)}, bf16[1,128,1024]{2,1,0:T(8,128)(2,1)}, bf16[1,128,1024]{2,1,0:T(8,128)(2,1)}) custom-call(bf16[1,128,1024]{2,1,0:T(8,128)(2,1)} %refs_0_.1, bf16[1,128,1024]{2,1,0:T(8,128)(2,1)} %refs_1_.1, bf16[1,128,1024]{2,1,0:T(8,128)(2,1)} %refs_2_.1, ...), custom_call_target="tpu_custom_call" | custom-call | tf_op jit(solution)/shard_map/pallas_call | solution.py:445
  81.3 0.0 copy-start.2
  81.3 1.9 %copy.13 = bf16[1,128,2048]{2,1,0:T(8,128)(2,1)} copy(bf16[1,128,2048]{2,1,0:T(8,128)(2,1)} %get-tuple-element.8) | data formatting | bytes 1048576
  83.2 0.0 copy-done.2
  83.2 0.0 copy-start.1
  83.2 0.7 copy.14
  83.9 0.3 copy-done.1
  84.3 0.0 copy-start
  84.3 0.7 copy.15
  85.0 0.3 copy-done
  85.3 0.7 copy.16
Async XLA Ops:
  81.3 1.9 %copy-start.2 = (bf16[1,128,1024]{2,1,0:T(8,128)(2,1)S(1)}, bf16[1,128,1024]{2,1,0:T(8,128)(2,1)}, u32[]{:S(2)}) copy-start(bf16[1,128,1024]{2,1,0:T(8,128)(2,1)} %get-tuple-element.9) | copy-start | bytes 786436
  83.2 1.0 %copy-start.1 = (bf16[1,128,1024]{2,1,0:T(8,128)(2,1)S(1)}, bf16[1,128,1024]{2,1,0:T(8,128)(2,1)}, u32[]{:S(2)}) copy-start(bf16[1,128,1024]{2,1,0:T(8,128)(2,1)} %get-tuple-element.10) | copy-start | bytes 786436
  84.3 1.0 %copy-start = (bf16[1,128,1024]{2,1,0:T(8,128)(2,1)S(1)}, bf16[1,128,1024]{2,1,0:T(8,128)(2,1)}, u32[]{:S(2)}) copy-start(bf16[1,128,1024]{2,1,0:T(8,128)(2,1)} %get-tuple-element.11) | copy-start | bytes 786436

commit v3 on v2

--- a/solution.py
+++ b/solution.py
@@ -174,36 +174,46 @@
     @pl.when(has_down)
     def _():
         pl.semaphore_signal(barrier, inc=1, device_id=down, device_id_type=MESH)
-    pl.semaphore_wait(barrier, 4 + has_up.astype(jnp.int32) + has_down.astype(jnp.int32))
+    partners = 4 + has_up.astype(jnp.int32) + has_down.astype(jnp.int32)
+    for far in (2, -2):
+        near = (z + far < nz) if far > 0 else (z + far >= 0)
+        partners += near.astype(jnp.int32)
+
+        @pl.when(near)
+        def _():
+            pl.semaphore_signal(
+                barrier, inc=1, device_id={"seq": jnp.clip(z + far, 0, nz - 1)}, device_id_type=MESH)
+    pl.semaphore_wait(barrier, partners)
 
     mine = w.at[:, pl.ds(pl.multiple_of(y * half, 128), half)]
     deep = feat // CHUNKS
 
-    def source(block, d, c):
-        held = mine if d == 0 else wg.at[block]
-        return held.at[c * deep:(c + 1) * deep]
-
-    def up_copy(block, d, c):
-        return remote(source(block, d, c), wg.at[block, c * deep:(c + 1) * deep], wu_s.at[d, c], wu_r.at[d, c], up)
-
-    def down_copy(block, d, c):
-        return remote(source(block, d, c), wg.at[block, c * deep:(c + 1) * deep], wd_s.at[d, c], wd_r.at[d, c], down)
+    def chunk(ref, c):
+        return ref.at[c * deep:(c + 1) * deep]
+
+    def far_copy(far, c):
+        block = wg.at[z]
+        i = 1 if far > 0 else 0
+        target = {"seq": jnp.clip(z + far, 0, nz - 1)}
+        return remote(chunk(mine, c), chunk(block, c), wu_s.at[abs(far) - 1, i, c], wu_r.at[abs(far) - 1, i, c], target)
+
+    def pass_copy(step, c):
+        block = wg.at[jnp.clip(z - 2 * step, 0, nz - 1)]
+        i = 1 if step > 0 else 0
+        return remote(chunk(block, c), chunk(block, c), wd_s.at[i, c], wd_r.at[i, c], up if step > 0 else down)
+
+    def within(far):
+        return (z + far < nz) if far > 0 else (z + far >= 0)
 
     def start_own(c):
-        @pl.when(has_up)
-        def _():
-            up_copy(z, 0, c).start()
-
-        @pl.when((z < nz - 1) & has_down)
-        def _():
-            down_copy(z, 0, c).start()
+        for far in (2, -2, 1, -1):
+            if abs(far) < nz:
+                @pl.when(within(far))
+                def _():
+                    far_copy(far, c).start()
 
     start_own(0)
-
-    @pl.when(z == nz - 1)
-    def _():
-        for c in range(CHUNKS):
-            down_copy(z, 0, c).start()
+    start_own(1)
     own_w = pltpu.make_async_copy(mine, wg.at[z], own_sem.at[nz])
     own_w.start()
 
@@ -302,24 +312,27 @@
             suffix_copy(g).start()
 
     for c in range(CHUNKS):
-        if c + 1 < CHUNKS:
-            start_own(c + 1)
-        for d in range(1, nz):
-            @pl.when(z - d >= 0)
+        if c + 2 < CHUNKS:
+            start_own(c + 2)
+        if nz > 2:
+            for step in (1, -1):
+                @pl.when(within(-2 * step))
+                def _():
+                    far_copy(2 * step, c).wait_recv()
+
+                if nz > 3:
+                    @pl.when(within(-2 * step) & within(step))
+                    def _():
+                        pass_copy(step, c).start()
+        for step in (1, -1):
+            @pl.when(within(-step))
             def _():
-                up_copy(z - d, d - 1, c).wait_recv()
-
-                @pl.when(has_up)
+                far_copy(step, c).wait_recv()
+
+            if nz > 3:
+                @pl.when(within(-3 * step))
                 def _():
-                    up_copy(z - d, d, c).start()
-
-            @pl.when(z + d < nz)
-            def _():
-                down_copy(z + d, d - 1, c).wait_recv()
-
-                @pl.when(has_down)
-                def _():
-                    down_copy(z + d, d, c).start()
+                    pass_copy(step, c).wait_recv()
         if c == 0:
             own_w.wait()
             for b in range(nz):
@@ -358,6 +371,20 @@
         osend[i] = dot(left, wg[(1 - s) * hb + i], 1, 0).astype(BF16).reshape(4, rows, half)
     sub_copy.start()
 
+    def hop():
+        for g in range(CHUNKS):
+            suffix_copy(g).wait_recv()
+
+            @pl.when(has_down)
+            def _():
+                part = slice(g * per, (g + 1) * per)
+                sout[part] = (sin[part].astype(F32) + lst[part]).astype(BF16)
+                suffix_copy(g).start()
+
+    @pl.when(z == nz - 2)
+    def _():
+        hop()
+
     @pl.loop(0, hb)
     def _(i):
         left = normg[...].reshape(4 * rows, feat)
@@ -370,17 +397,6 @@
         kloc[h] = dot(grad_scores, q[0, :, col(h)], 0, 0)
         vloc[h] = dot(scores[h], turned, 0, 0)
 
-    @pl.when(has_up)
-    def _():
-        for g in range(CHUNKS):
-            suffix_copy(g).wait_recv()
-
-            @pl.when(has_down)
-            def _():
-                part = slice(g * per, (g + 1) * per)
-                sout[part] = (sin[part].astype(F32) + lst[part]).astype(BF16)
-                suffix_copy(g).start()
-
     def out_copy(i, j):
         return remote(ofin.at[i, j], oin.at[i, j], f_s.at[i, j], f_r.at[i, j], to_peer(j))
 
@@ -389,6 +405,10 @@
         ofin[i] = (oacc[i] + orecv[i].astype(F32)).astype(BF16)
         for j in (1, 2, 3):
             out_copy(i, j).start()
+
+    @pl.when(z < nz - 2)
+    def _():
+        hop()
 
     for h in range(head_count):
         kg[0, :, col(h)] = (kloc[h] + dot(v[0, :, col(h)], sin[h], 1, 1)).astype(BF16)
@@ -405,14 +425,17 @@
                 out[0, :, part] = oin[i, j]
 
     for c in range(CHUNKS):
-        for d in range(nz - 1):
-            @pl.when(has_up & (z - d >= 0))
-            def _():
-                up_copy(z, d, c).wait_send()
-
-            @pl.when(has_down & (z + d < nz))
-            def _():
-                down_copy(z, d, c).wait_send()
+        for far in (2, -2, 1, -1):
+            if abs(far) < nz:
+                @pl.when(within(far))
+                def _():
+                    far_copy(far, c).wait_send()
+
+        if nz > 3:
+            for step in (1, -1):
+                @pl.when(within(-2 * step) & within(step))
+                def _():
+                    pass_copy(step, c).wait_send()
 
     for g in range(CHUNKS):
         @pl.when(has_up)
@@ -458,12 +481,12 @@
             vmem((heads, rows, HS), BF16), vmem((heads, rows, HS), F32), vmem((heads, rows, HS), F32),
             vmem(states, BF16), vmem(states, BF16),
             vmem((1, rows, feat), BF16), vmem((1, rows, feat), BF16), vmem((1, rows, feat), BF16), dma((3,)),
-            dma((nz + 1,)), dma((nz, CHUNKS)), dma((nz, CHUNKS)), dma((nz, CHUNKS)), dma((nz, CHUNKS)),
+            dma((nz + 1,)), dma((2, 2, CHUNKS)), dma((2, 2, CHUNKS)), dma((2, CHUNKS)), dma((2, CHUNKS)),
             dma((4, nz)), dma((4, nz)), dma((CHUNKS,)), dma((CHUNKS,)), dma((CHUNKS,)), dma((CHUNKS,)),
             dma((4,)), dma((4,)), dma((4, CHUNKS)), dma((4, CHUNKS)), dma((1,)), dma((1,)), dma((hb, 4)), dma((hb, 4)),
         ],
         compiler_params=pltpu.CompilerParams(
-            collective_id=0, has_side_effects=True, vmem_limit_bytes=60 * 1024 * 1024),
+            collective_id=0, has_side_effects=True, vmem_limit_bytes=55 * 1024 * 1024),
     )(queries, key_vectors, value_vectors, out_weight, out_cotangent))
 
 

time: 86.2 us -> 88.2 us (1.023)
  Pallas kernels: 80.7 us -> 82.6 us
    pallas_call x1, Pallas kernels: 80.7 us -> 82.6 us  [fused(): pl.pallas_call(functools.partial(body, nz, heads, rows, wd), out_shape=(j...]
where the time goes in v3:
time: 88.2 us; the launch traced here: 88 us
  Pallas kernels  82.6 us (94%)
  local copies, waits for them, and re-layouts  4.72 us (5%)
    pallas_call x1, Pallas kernels, fused(): pl.pallas_call(functools.partial(body, nz, heads, rows, wd), out_shape=(j...  82.6 us
    unnamed x10, local copies, waits for them, and re-layouts  4.72 us

profile of v3, /device:TPU:0, one launch (start us, length us, event | category | flops | bytes accessed | tf_op | source)
XLA Modules:
  0.0 88.0 jit_solution(9840161408299840505)
XLA Ops:
  0.6 82.6 %shard_map.84 = (bf16[1,128,2048]{2,1,0:T(8,128)(2,1)}, bf16[1,128,1024]{2,1,0:T(8,128)(2,1)}, bf16[1,128,1024]{2,1,0:T(8,128)(2,1)}, bf16[1,128,1024]{2,1,0:T(8,128)(2,1)}) custom-call(bf16[1,128,1024]{2,1,0:T(8,128)(2,1)} %refs_0_.1, bf16[1,128,1024]{2,1,0:T(8,128)(2,1)} %refs_1_.1, bf16[1,128,1024]{2,1,0:T(8,128)(2,1)} %refs_2_.1, ...), custom_call_target="tpu_custom_call" | custom-call | tf_op jit(solution)/shard_map/pallas_call | solution.py:468
  83.3 0.0 copy-start.2
  83.3 1.9 %copy.13 = bf16[1,128,2048]{2,1,0:T(8,128)(2,1)} copy(bf16[1,128,2048]{2,1,0:T(8,128)(2,1)} %get-tuple-element.8) | data formatting | bytes 1048576
  85.2 0.0 copy-done.2
  85.2 0.0 copy-start.1
  85.2 0.7 copy.14
  85.9 0.3 copy-done.1
  86.3 0.0 copy-start
  86.3 0.7 copy.15
  87.0 0.3 copy-done
  87.3 0.7 copy.16
Async XLA Ops:
  83.3 1.9 %copy-start.2 = (bf16[1,128,1024]{2,1,0:T(8,128)(2,1)S(1)}, bf16[1,128,1024]{2,1,0:T(8,128)(2,1)}, u32[]{:S(2)}) copy-start(bf16[1,128,1024]{2,1,0:T(8,128)(2,1)} %get-tuple-element.9) | copy-start | bytes 786436
  85.2 1.0 %copy-start.1 = (bf16[1,128,1024]{2,1,0:T(8,128)(2,1)S(1)}, bf16[1,128,1024]{2,1,0:T(8,128)(2,1)}, u32[]{:S(2)}) copy-start(bf16[1,128,1024]{2,1,0:T(8,128)(2,1)} %get-tuple-element.10) | copy-start | bytes 786436
  86.3 1.0 %copy-start = (bf16[1,128,1024]{2,1,0:T(8,128)(2,1)S(1)}, bf16[1,128,1024]{2,1,0:T(8,128)(2,1)}, u32[]{:S(2)}) copy-start(bf16[1,128,1024]{2,1,0:T(8,128)(2,1)} %get-tuple-element.11) | copy-start | bytes 786436

commit v4 on v2

--- a/solution.py
+++ b/solution.py
@@ -345,7 +345,7 @@
         if c == CHUNKS - 2:
             turn(0)
         if c == CHUNKS - 1:
-            for g in range(1, CHUNKS):
+            for g in range(1, CHUNKS - 1):
                 turn(g)
 
     for j in (1, 2, 3):
@@ -362,6 +362,17 @@
     def _(i):
         left = normg[...].reshape(4 * rows, feat)
         oacc[i] = dot(left, wg[s * hb + i], 1, 0).reshape(4, rows, half)
+
+    turn(CHUNKS - 1)
+
+    def out_copy(i, j):
+        return remote(ofin.at[i, j], oin.at[i, j], f_s.at[i, j], f_r.at[i, j], to_peer(j))
+
+    sub_copy.wait_recv()
+    for i in range(hb):
+        ofin[i] = (oacc[i] + orecv[i].astype(F32)).astype(BF16)
+        for j in (1, 2, 3):
+            out_copy(i, j).start()
 
     for h in range(head_count):
         turned = ag[h]
@@ -380,15 +391,6 @@
                 part = slice(g * per, (g + 1) * per)
                 sout[part] = (sin[part].astype(F32) + lst[part]).astype(BF16)
                 suffix_copy(g).start()
-
-    def out_copy(i, j):
-        return remote(ofin.at[i, j], oin.at[i, j], f_s.at[i, j], f_r.at[i, j], to_peer(j))
-
-    sub_copy.wait_recv()
-    for i in range(hb):
-        ofin[i] = (oacc[i] + orecv[i].astype(F32)).astype(BF16)
-        for j in (1, 2, 3):
-            out_copy(i, j).start()
 
     for h in range(head_count):
         kg[0, :, col(h)] = (kloc[h] + dot(v[0, :, col(h)], sin[h], 1, 1)).astype(BF16)

time: 86.2 us -> 81.1 us (0.941)
  Pallas kernels: 80.7 us -> 75.5 us
    pallas_call x1, Pallas kernels: 80.7 us -> 75.5 us  [fused(): pl.pallas_call(functools.partial(body, nz, heads, rows, wd), out_shape=(j...]
where the time goes in v4:
time: 81.1 us; the launch traced here: 80.9 us
  Pallas kernels  75.5 us (93%)
  local copies, waits for them, and re-layouts  4.72 us (6%)
    pallas_call x1, Pallas kernels, fused(): pl.pallas_call(functools.partial(body, nz, heads, rows, wd), out_shape=(j...  75.5 us
    unnamed x10, local copies, waits for them, and re-layouts  4.72 us

profile of v4, /device:TPU:0, one launch (start us, length us, event | category | flops | bytes accessed | tf_op | source)
XLA Modules:
  0.0 80.9 jit_solution(10923438268276892749)
XLA Ops:
  0.6 75.5 %shard_map.84 = (bf16[1,128,2048]{2,1,0:T(8,128)(2,1)}, bf16[1,128,1024]{2,1,0:T(8,128)(2,1)}, bf16[1,128,1024]{2,1,0:T(8,128)(2,1)}, bf16[1,128,1024]{2,1,0:T(8,128)(2,1)}) custom-call(bf16[1,128,1024]{2,1,0:T(8,128)(2,1)} %refs_0_.1, bf16[1,128,1024]{2,1,0:T(8,128)(2,1)} %refs_1_.1, bf16[1,128,1024]{2,1,0:T(8,128)(2,1)} %refs_2_.1, ...), custom_call_target="tpu_custom_call" | custom-call | tf_op jit(solution)/shard_map/pallas_call | solution.py:447
  76.1 0.0 copy-start.2
  76.1 1.9 %copy.13 = bf16[1,128,2048]{2,1,0:T(8,128)(2,1)} copy(bf16[1,128,2048]{2,1,0:T(8,128)(2,1)} %get-tuple-element.8) | data formatting | bytes 1048576
  78.1 0.0 copy-done.2
  78.1 0.0 copy-start.1
  78.1 0.7 copy.14
  78.8 0.3 copy-done.1
  79.1 0.0 copy-start
  79.1 0.7 copy.15
  79.8 0.3 copy-done
  80.2 0.7 copy.16
Async XLA Ops:
  76.1 1.9 %copy-start.2 = (bf16[1,128,1024]{2,1,0:T(8,128)(2,1)S(1)}, bf16[1,128,1024]{2,1,0:T(8,128)(2,1)}, u32[]{:S(2)}) copy-start(bf16[1,128,1024]{2,1,0:T(8,128)(2,1)} %get-tuple-element.9) | copy-start | bytes 786436
  78.1 1.0 %copy-start.1 = (bf16[1,128,1024]{2,1,0:T(8,128)(2,1)S(1)}, bf16[1,128,1024]{2,1,0:T(8,128)(2,1)}, u32[]{:S(2)}) copy-start(bf16[1,128,1024]{2,1,0:T(8,128)(2,1)} %get-tuple-element.10) | copy-start | bytes 786436
  79.1 1.0 %copy-start = (bf16[1,128,1024]{2,1,0:T(8,128)(2,1)S(1)}, bf16[1,128,1024]{2,1,0:T(8,128)(2,1)}, u32[]{:S(2)}) copy-start(bf16[1,128,1024]{2,1,0:T(8,128)(2,1)} %get-tuple-element.11) | copy-start | bytes 786436

commit v5 on v4

--- a/solution.py
+++ b/solution.py
@@ -374,6 +374,20 @@
         for j in (1, 2, 3):
             out_copy(i, j).start()
 
+    def hop():
+        for g in range(CHUNKS):
+            suffix_copy(g).wait_recv()
+
+            @pl.when(has_down)
+            def _():
+                part = slice(g * per, (g + 1) * per)
+                sout[part] = (sin[part].astype(F32) + lst[part]).astype(BF16)
+                suffix_copy(g).start()
+
+    @pl.when(z == nz - 2)
+    def _():
+        hop()
+
     for h in range(head_count):
         turned = ag[h]
         grad_scores = jnp.where(causal, dot(turned, v[0, :, col(h)], 1, 1), 0.0).astype(BF16)
@@ -381,16 +395,9 @@
         kloc[h] = dot(grad_scores, q[0, :, col(h)], 0, 0)
         vloc[h] = dot(scores[h], turned, 0, 0)
 
-    @pl.when(has_up)
+    @pl.when(z < nz - 2)
     def _():
-        for g in range(CHUNKS):
-            suffix_copy(g).wait_recv()
-
-            @pl.when(has_down)
-            def _():
-                part = slice(g * per, (g + 1) * per)
-                sout[part] = (sin[part].astype(F32) + lst[part]).astype(BF16)
-                suffix_copy(g).start()
+        hop()
 
     for h in range(head_count):
         kg[0, :, col(h)] = (kloc[h] + dot(v[0, :, col(h)], sin[h], 1, 1)).astype(BF16)

time: 81.1 us -> 81.1 us (level)
  no operation moved by 1% of the time
where the time goes in v5:
time: 81.1 us; the launch traced here: 80.9 us
  Pallas kernels  75.5 us (93%)
  local copies, waits for them, and re-layouts  4.72 us (6%)
    pallas_call x1, Pallas kernels, fused(): pl.pallas_call(functools.partial(body, nz, heads, rows, wd), out_shape=(j...  75.5 us
    unnamed x10, local copies, waits for them, and re-layouts  4.72 us

profile of v5, /device:TPU:0, one launch (start us, length us, event | category | flops | bytes accessed | tf_op | source)
XLA Modules:
  0.0 80.9 jit_solution(969393704664169789)
XLA Ops:
  0.6 75.5 %shard_map.84 = (bf16[1,128,2048]{2,1,0:T(8,128)(2,1)}, bf16[1,128,1024]{2,1,0:T(8,128)(2,1)}, bf16[1,128,1024]{2,1,0:T(8,128)(2,1)}, bf16[1,128,1024]{2,1,0:T(8,128)(2,1)}) custom-call(bf16[1,128,1024]{2,1,0:T(8,128)(2,1)} %refs_0_.1, bf16[1,128,1024]{2,1,0:T(8,128)(2,1)} %refs_1_.1, bf16[1,128,1024]{2,1,0:T(8,128)(2,1)} %refs_2_.1, ...), custom_call_target="tpu_custom_call" | custom-call | tf_op jit(solution)/shard_map/pallas_call | solution.py:454
  76.1 0.0 copy-start.2
  76.1 1.9 %copy.13 = bf16[1,128,2048]{2,1,0:T(8,128)(2,1)} copy(bf16[1,128,2048]{2,1,0:T(8,128)(2,1)} %get-tuple-element.8) | data formatting | bytes 1048576
  78.1 0.0 copy-done.2
  78.1 0.0 copy-start.1
  78.1 0.7 copy.14
  78.8 0.3 copy-done.1
  79.1 0.0 copy-start
  79.1 0.7 copy.15
  79.8 0.3 copy-done
  80.2 0.7 copy.16
Async XLA Ops:
  76.1 1.9 %copy-start.2 = (bf16[1,128,1024]{2,1,0:T(8,128)(2,1)S(1)}, bf16[1,128,1024]{2,1,0:T(8,128)(2,1)}, u32[]{:S(2)}) copy-start(bf16[1,128,1024]{2,1,0:T(8,128)(2,1)} %get-tuple-element.9) | copy-start | bytes 786436
  78.1 1.0 %copy-start.1 = (bf16[1,128,1024]{2,1,0:T(8,128)(2,1)S(1)}, bf16[1,128,1024]{2,1,0:T(8,128)(2,1)}, u32[]{:S(2)}) copy-start(bf16[1,128,1024]{2,1,0:T(8,128)(2,1)} %get-tuple-element.10) | copy-start | bytes 786436
  79.1 1.0 %copy-start = (bf16[1,128,1024]{2,1,0:T(8,128)(2,1)S(1)}, bf16[1,128,1024]{2,1,0:T(8,128)(2,1)}, u32[]{:S(2)}) copy-start(bf16[1,128,1024]{2,1,0:T(8,128)(2,1)} %get-tuple-element.11) | copy-start | bytes 786436
